TPU v7x, 256 devices: a whole 4x4x8 slice. The times are simulated.
256 devices in a mesh: panel: 32 (over z, y_lo, core), rep: 8 (over x, y_hi).
Axes of the slice: x: 4, y: 4 (y_hi: 2, y_lo: 2; y = y_hi * 2 + y_lo), z: 8, core: 2. Of those that a mesh axis runs over, the one named last changes fastest.
Arguments:
- x_src: bfloat16 [4096, 128], P('panel'), may hold values from -6 to 6
- x_dst: bfloat16 [131072, 128], P(('panel', 'rep')), may hold values from -6 to 6
- weight: bfloat16 [128, 512], replicated, may hold values from -0.5 to 0.5
- att_src: float32 [8, 64], replicated, may hold values from -0.75 to 0.75
- att_dst: float32 [8, 64], replicated, may hold values from -0.75 to 0.75
- grad_out: bfloat16 [131072, 512], P(('panel', 'rep')), may hold values from -6 to 6
- block_rows: int32 [4096], P(('panel', 'rep')), may hold values from 0 to 3, as said below
- block_cols: int32 [4096], P(('panel', 'rep')), may hold values from 0 to 31
- block_masks: int32 [4096, 128, 128], P(('panel', 'rep')), may hold values from 0 to 1, as said below
- block_counts: int32 [256], P(('panel', 'rep')), may hold values from 2 to 16, as said below
Outputs:
- grad_src: float32 [4096, 128], P('panel')
- grad_dst: float32 [131072, 128], P(('panel', 'rep'))
- grad_weight: float32 [128, 512], replicated
- grad_att_src: float32 [8, 64], replicated
- grad_att_dst: float32 [8, 64], replicated
Inputs may be any that keep to these rules, and one draw needn't show every extreme that they name: `block_counts`: live block slots of one device; at least one device has exactly 16. The pairs of block_rows and block_cols within one device's 16 slots are distinct. `block_masks`: slots at or after a device's count of live blocks hold only zeros.
All inputs are finite; a program needn't handle non-finite values.
Results may differ from a plain program's by a relative error of at most 0.012.
The roundings to bfloat16 on the way count: a program that leaves them out, or rounds other values in their place, can miss the bound.
Values may be sent and summed in bfloat16 or wider, within the bound.
No kernel may reach another device: no remote copies, remote signals or barrier semaphores. Data moves between devices by JAX's collectives and lax.ppermute only.
A program may use at most 128 MiB of HBM per device.

v0:
```python
import math
import jax
import jax.numpy as jnp
from jax import lax
from jax.sharding import PartitionSpec as P

HIGHEST_PRECISION = lax.Precision.HIGHEST


def smooth_leaky(values):
    return 0.2 * values + 0.8 * jax.nn.softplus(values)


def smooth_slope(values):
    return 0.2 + 0.8 * jax.nn.sigmoid(values)


def shards(
    x_src,
    x_dst,
    weight,
    att_src,
    att_dst,
    grad_out,
    block_rows,
    block_cols,
    block_masks,
    block_counts,
):
    num_heads, head_dim = att_src.shape
    model_width = weight.shape[1]
    block_size = block_masks.shape[1]
    dest_count = x_dst.shape[0]
    source_local = x_src.shape[0]
    slot_count = block_rows.shape[0]
    proj_own = jnp.dot(x_src, weight, preferred_element_type=jnp.float32).astype(jnp.bfloat16)
    proj_all = lax.all_gather(proj_own, "panel", axis=0, tiled=True)
    source_total = proj_all.shape[0]
    dest_blocks = dest_count // block_size
    source_blocks = source_total // block_size
    source_feats = proj_all.reshape(source_total, num_heads, head_dim)
    score_src = jnp.einsum(
        "jhk,hk->hj", source_feats.astype(jnp.float32), att_src, precision=HIGHEST_PRECISION
    )
    proj_dst = jnp.dot(x_dst, weight, preferred_element_type=jnp.float32).astype(jnp.bfloat16)
    feats = proj_dst.reshape(dest_count, num_heads, head_dim)
    feats_wide = feats.astype(jnp.float32)
    score_d = jnp.einsum("ihk,hk->hi", feats_wide, att_dst, precision=HIGHEST_PRECISION)
    score_own = jnp.einsum("ihk,hk->hi", feats_wide, att_src, precision=HIGHEST_PRECISION)
    cotan = grad_out.reshape(dest_count, num_heads, head_dim)
    cotan_wide = cotan.astype(jnp.float32)
    live_count = block_counts[0]
    score_d_blocks = score_d.reshape(num_heads, dest_blocks, block_size)
    score_src_blocks = score_src.reshape(num_heads, source_blocks, block_size)
    source_row_blocks = source_feats.reshape(source_blocks, block_size, num_heads, head_dim)
    cotan_blocks = cotan.reshape(dest_blocks, block_size, num_heads, head_dim)
    group = math.gcd(slot_count, 16)
    groups = slot_count // group
    alive_all = (jnp.arange(slot_count, dtype=jnp.int32) < live_count).astype(jnp.float32)
    slot_inputs = (
        block_rows.reshape(groups, group),
        block_cols.reshape(groups, group),
        block_masks.reshape(groups, group, block_size, block_size),
        alive_all.reshape(groups, group),
    )

    def group_scores(rows, cols, masks, alive):
        dest_hot = (rows[:, None] == jnp.arange(dest_blocks, dtype=jnp.int32)[None, :]).astype(
            jnp.float32
        )
        source_hot = (cols[:, None] == jnp.arange(source_blocks, dtype=jnp.int32)[None, :]).astype(
            jnp.float32
        )
        score_rows = jnp.einsum(
            "gd,hdu->ghu", dest_hot, score_d_blocks, precision=HIGHEST_PRECISION
        )
        score_cols = jnp.einsum(
            "gs,hsv->ghv", source_hot, score_src_blocks, precision=HIGHEST_PRECISION
        )
        pre_score = score_rows[:, :, :, None] + score_cols[:, :, None, :]
        edge_mask = masks.astype(jnp.float32) * alive[:, None, None]
        edge_weight = jnp.exp(smooth_leaky(pre_score)) * edge_mask[:, None]
        source_rows = jnp.take(source_row_blocks, cols, axis=0)
        return (dest_hot, source_hot, pre_score, edge_weight, source_rows)

    def forward_group(carried_fwd, slot_group):
        denominator, numerator = carried_fwd
        rows, cols, masks, alive = slot_group
        dest_hot, source_hot, pre_score, edge_weight, source_rows = group_scores(
            rows, cols, masks, alive
        )
        part_num = jnp.einsum(
            "ghij,gjhk->gihk",
            edge_weight.astype(jnp.bfloat16),
            source_rows,
            preferred_element_type=jnp.float32,
        )
        denominator = denominator + jnp.einsum(
            "gd,ghi->hdi", dest_hot, edge_weight.sum(axis=3), precision=HIGHEST_PRECISION
        )
        numerator = numerator + jnp.einsum(
            "gd,gihk->dihk", dest_hot, part_num, precision=HIGHEST_PRECISION
        )
        return ((denominator, numerator), None)

    (denominator_blocks, numerator_blocks), _ = lax.scan(
        forward_group,
        (
            jnp.zeros((num_heads, dest_blocks, block_size), jnp.float32),
            jnp.zeros((dest_blocks, block_size, num_heads, head_dim), jnp.float32),
        ),
        slot_inputs,
    )
    denominator = denominator_blocks.reshape(num_heads, dest_count)
    numerator = numerator_blocks.reshape(dest_count, num_heads, head_dim)
    pre_self = score_d + score_own
    self_weight = jnp.exp(smooth_leaky(pre_self))
    denominator = denominator + self_weight
    numerator = numerator + self_weight.T[:, :, None] * feats_wide
    attended = numerator / denominator.T[:, :, None]
    centred = jnp.sum(cotan_wide * attended, axis=2).T
    denominator_full = denominator.reshape(num_heads, dest_blocks, block_size)
    centred_full = centred.reshape(num_heads, dest_blocks, block_size)

    def backward_group(carried_bwd, slot_group):
        grad_source, grad_score_src, grad_score_dst = carried_bwd
        rows, cols, masks, alive = slot_group
        dest_hot, source_hot, pre_score, edge_weight, source_rows = group_scores(
            rows, cols, masks, alive
        )
        denom_rows = jnp.einsum(
            "gd,hdi->ghi", dest_hot, denominator_full, precision=HIGHEST_PRECISION
        )
        attention = edge_weight / denom_rows[:, :, :, None]
        cotan_rows = jnp.take(cotan_blocks, rows, axis=0)
        pair_grad = jnp.einsum(
            "gihk,gjhk->ghij", cotan_rows, source_rows, preferred_element_type=jnp.float32
        )
        centred_rows = jnp.einsum(
            "gd,hdi->ghi", dest_hot, centred_full, precision=HIGHEST_PRECISION
        )
        score_grad = attention * (pair_grad - centred_rows[:, :, :, None]) * smooth_slope(pre_score)
        feat_grad = jnp.einsum(
            "ghij,gihk->gjhk",
            attention.astype(jnp.bfloat16),
            cotan_rows,
            preferred_element_type=jnp.float32,
        )
        grad_source = grad_source + jnp.einsum(
            "gs,gjhk->sjhk", source_hot, feat_grad, precision=HIGHEST_PRECISION
        )
        grad_score_src = grad_score_src + jnp.einsum(
            "gs,ghj->hsj", source_hot, score_grad.sum(axis=2), precision=HIGHEST_PRECISION
        )
        grad_score_dst = grad_score_dst + jnp.einsum(
            "gd,ghi->hdi", dest_hot, score_grad.sum(axis=3), precision=HIGHEST_PRECISION
        )
        return ((grad_source, grad_score_src, grad_score_dst), None)

    (grad_source_blocks, grad_score_src_blocks, grad_score_dst_blocks), _ = lax.scan(
        backward_group,
        (
            jnp.zeros((source_blocks, block_size, num_heads, head_dim), jnp.float32),
            jnp.zeros((num_heads, source_blocks, block_size), jnp.float32),
            jnp.zeros((num_heads, dest_blocks, block_size), jnp.float32),
        ),
        slot_inputs,
    )
    grad_source = grad_source_blocks.reshape(source_total, num_heads, head_dim)
    grad_score_src = grad_score_src_blocks.reshape(num_heads, source_total)
    grad_score_dst = grad_score_dst_blocks.reshape(num_heads, dest_count)
    self_attention = self_weight / denominator
    self_pair = jnp.sum(cotan_wide * feats_wide, axis=2).T
    self_grad = self_attention * (self_pair - centred) * smooth_slope(pre_self)
    grad_score_dst = grad_score_dst + self_grad
    grad_dest = (
        self_attention.T[:, :, None] * cotan_wide
        + self_grad.T[:, :, None] * att_src[None]
        + grad_score_dst.T[:, :, None] * att_dst[None]
    )
    grad_source = grad_source + grad_score_src.T[:, :, None] * att_src[None]
    att_src_part = jnp.einsum(
        "hj,jhk->hk", grad_score_src, source_feats.astype(jnp.float32), precision=HIGHEST_PRECISION
    ) + jnp.einsum("hi,ihk->hk", self_grad, feats_wide, precision=HIGHEST_PRECISION)
    att_dst_part = jnp.einsum("hi,ihk->hk", grad_score_dst, feats_wide, precision=HIGHEST_PRECISION)
    weight_t = weight.astype(jnp.float32).T
    source_flat = grad_source.reshape(source_total, model_width)
    dest_flat = grad_dest.reshape(dest_count, model_width)
    grad_dst = jnp.dot(dest_flat, weight_t, precision=HIGHEST_PRECISION)
    weight_part = jnp.dot(x_dst.astype(jnp.float32).T, dest_flat, precision=HIGHEST_PRECISION)
    share_rows = source_local // lax.axis_size("rep")
    share_start = lax.axis_index("rep") * share_rows
    panel_part = lax.psum_scatter(source_flat, "panel", scatter_dimension=0, tiled=True)
    panel_sum = lax.psum(panel_part, "rep")
    own_share = lax.dynamic_slice_in_dim(panel_sum, share_start, share_rows, 0)
    grad_src = jnp.dot(panel_sum, weight_t, precision=HIGHEST_PRECISION)
    own_inputs = lax.dynamic_slice_in_dim(x_src, share_start, share_rows, 0).astype(jnp.float32)
    weight_part = weight_part + jnp.dot(own_inputs.T, own_share, precision=HIGHEST_PRECISION)
    grad_weight, grad_att_src, grad_att_dst = lax.psum(
        (weight_part, att_src_part, att_dst_part), ("panel", "rep")
    )
    return (grad_src, grad_dst, grad_weight, grad_att_src, grad_att_dst)


def solution(mesh):
    return jax.shard_map(
        shards,
        mesh=mesh,
        in_specs=(
            P("panel", None),
            P(("panel", "rep"), None),
            P(),
            P(),
            P(),
            P(("panel", "rep"), None),
            P(("panel", "rep")),
            P(("panel", "rep")),
            P(("panel", "rep"), None, None),
            P(("panel", "rep")),
        ),
        out_specs=(P("panel", None), P(("panel", "rep"), None), P(), P(), P()),
        check_vma=False,
    )
```

profile of v0, /device:TPU:2, one launch (start us, length us, event | category | flops | bytes accessed | tf_op | source)
XLA Modules:
  0.0 674.6 jit_solution(18316904664663348412)
XLA Ops:
  9.7 2.1 copy.48
  20.7 2.4 convert_multiply_fusion.2
  23.1 57.2 %all-gather.2.cloned.1.call-done = bf16[4096,512]{1,0:T(8,128)(2,1)} async-done(((bf16[128,512]{1,0:T(8,128)(2,1)}), bf16[4096,512]{1,0:T(8,128)(2,1)}) %all-gather.2.cloned.1.call-update) | async-done | bytes 4194320 | tf_op jit(solution)/shard_map/all_gather | solution.py:37
  80.3 6.4 copy.41
  86.7 3.9 fusion.99
  91.0 9.5 %fusion.23 = f32[16,8,128]{2,1,0:T(8,128)S(1)} fusion(f32[16,128,128]{2,1,0:T(8,128)} %convert_multiply_fusion.2, f32[16,8,128]{2,1,0:T(8,128)S(1)} %copy.42, f32[16,8,128]{2,1,0:T(8,128)S(1)} %copy.40), kind=kLoop, calls=%fused_computation.33 | loop fusion | flops 25149440 | bytes 1245184 | tf_op jit(solution)/shard_map/while/body/eval_jaxpr/reduce_sum | solution.py:99
  100.7 11.2 %reshape.149 = bf16[32,128,8,64]{3,2,1,0:T(8,128)(2,1)} reshape(bf16[4096,512]{1,0:T(8,128)(2,1)} %all-gather.2.cloned.1.call-done) | data formatting | bytes 8388608 | tf_op jit(solution)/shard_map/reshape;reshape | solution.py:55
  111.8 9.1 %copy.47 = bf16[32,128,8,64]{1,3,2,0:T(8,128)(2,1)} copy(bf16[32,128,8,64]{3,2,1,0:T(8,128)(2,1)} %reshape.149) | data formatting | bytes 8388608 | tf_op jit(solution)/shard_map/reshape;reshape | solution.py:55
  120.9 4.3 gather_fusion.1
  125.3 9.9 %fusion.27 = f32[16,128,8,64]{1,3,2,0:T(8,128)S(1)} fusion(f32[16,128,128]{2,1,0:T(8,128)} %convert_multiply_fusion.2, f32[16,8,128]{2,1,0:T(8,128)S(1)} %copy.42, f32[16,8,128]{2,1,0:T(8,128)S(1)} %copy.40, bf16[16,128,8,64]{1,3,2,0:T(8,128)(2,1)} %gather_fusion.1, pred[16]{0:T(512)(128)(4,1)S(1)} %get-tuple-element.104), kind=kOutput, calls=%fused_computation.35 | convolution fusion | flops 294649856 | bytes 7471120 | tf_op jit(solution)/shard_map/while/body/eval_jaxpr/ghij,gjhk->gihk/dot_general | solution.py:92
  135.1 5.0 fusion.14
  140.1 2.6 reshape.108
  144.9 11.8 %fusion.24 = f32[16,128,8,64]{1,3,2,0:T(8,128)S(1)} fusion(f32[16,8,128]{2,1,0:T(8,128)S(1)} %copy.44, f32[16,128,128]{2,1,0:T(8,128)} %convert_multiply_fusion.2, f32[16,8,128]{2,1,0:T(8,128)S(1)} %copy.42, f32[16,8,128]{2,1,0:T(8,128)S(1)} %copy.40, bf16[16,128,8,64]{1,3,2,0:T(8,128)(2,1)S(1)} %gather_fusion, pred[16]{0:T(512)(128)(4,1)S(1)} %get-tuple-element.105), kind=kOutput, calls=%fused_computation.34 | convolution fusion | flops 296747008 | bytes 7536656 | tf_op jit(solution)/shard_map/while/body/eval_jaxpr/ghij,gihk->gjhk/dot_general | solution.py:143
  156.7 15.4 %fusion.96 = (f32[16,8,128]{2,1,0:T(8,128)S(1)}, f32[16,8,128]{2,1,0:T(8,128)S(1)}) fusion(f32[16,8,128]{2,1,0:T(8,128)S(1)} %copy.50, bf16[16,128,8,64]{1,3,2,0:T(8,128)(2,1)S(1)} %copy-done.1, pred[16]{0:T(512)(128)(4,1)S(1)} %get-tuple-element.104, bf16[16,128,8,64]{1,3,2,0:T(8,128)(2,1)S(1)} %gather_fusion, pred[16]{0:T(512)(128)(4,1)S(1)} %get-tuple-element.105, ...), kind=kOutput, calls=%fused_computation.128 | convolution fusion | flops 316637184 | bytes 5636128 | tf_op jit(solution)/shard_map/while/body/eval_jaxpr/gihk,gjhk->ghij/dot_general | solution.py:136
  172.6 5.8 fusion.16
  178.4 12.0 %bitcast_add_fusion = f32[4096,512]{0,1:T(8,128)} fusion(f32[64,8,32,128]{3,2,1,0:T(8,128)S(1)} %bitcast.176, f32[512]{0:T(512)S(1)} %mul.185, f32[4096,8]{0,1:T(8,128)S(1)} %bitcast.183), kind=kLoop, calls=%fused_computation.22 | loop fusion | flops 4194304 | bytes 16910336 | tf_op jit(solution)/shard_map/add | solution.py:181
  192.9 5.1 fusion.103
  198.0 122.5 %reduce-scatter.2.cloned.1.call-done = f32[128,512]{0,1:T(8,128)} async-done(((f32[4096,512]{0,1:T(8,128)}), f32[128,512]{0,1:T(8,128)}) %reduce-scatter.2.cloned.1.call-update) | async-done | bytes 262160 | tf_op jit(solution)/shard_map/reduce_scatter | solution.py:193
  321.0 75.9 %all-reduce = (f32[8,64]{1,0:T(8,128)}, f32[8,64]{1,0:T(8,128)}) all-reduce(f32[8,64]{1,0:T(8,128)S(1)} %add.168, f32[8,64]{1,0:T(8,128)S(1)} %bitcast.197), channel_id=1, replica_groups=mesh['panel'=32,'rep'=8] {'panel','rep'}, use_global_device_ids=true, to_apply=%region_8.10 | all-reduce | flops 1024 | bytes 8192 | tf_op jit(solution)/shard_map/psum | solution.py:199
  398.6 11.2 %all-reduce.4.cloned.1.call-done = f32[128,512]{0,1:T(8,128)} async-done(((f32[128,512]{0,1:T(8,128)}), f32[128,512]{0,1:T(8,128)}) %all-reduce.4.cloned.1.call-update) | async-done | bytes 262160 | tf_op jit(solution)/shard_map/psum | solution.py:194
  409.9 2.0 convolution_add_fusion
  411.9 2.0 fusion.101
  413.8 252.2 %all-reduce.6.cloned.1.call-done = f32[128,512]{0,1:T(8,128)} async-done(((f32[128,512]{0,1:T(8,128)}), f32[128,512]{0,1:T(8,128)}) %all-reduce.6.cloned.1.call-update) | async-done | bytes 262160 | tf_op jit(solution)/shard_map/psum | solution.py:199
  666.1 1.8 copy.54
  (71 shorter events, 18.4 us)
Async XLA Ops:
  7.2 0.9 copy-start
  7.2 13.2 %copy-start.7 = (s32[16]{0:T(128)S(1)}, s32[16]{0:T(128)}, u32[]{:S(2)}) copy-start(s32[16]{0:T(128)} %param.18) | copy-start | bytes 196
  7.2 13.2 %copy-start.6 = (f32[8,64]{1,0:T(8,128)S(1)}, f32[8,64]{1,0:T(8,128)}, u32[]{:S(2)}) copy-start(f32[8,64]{1,0:T(8,128)} %param.15) | copy-start | bytes 6148
  7.2 13.1 %copy-start.9 = (s32[16]{0:T(128)S(1)}, s32[16]{0:T(128)}, u32[]{:S(2)}) copy-start(s32[16]{0:T(128)} %param.19) | copy-start | bytes 196
  7.2 73.1 %all-gather.2.cloned.1.call-start = ((), (), s32[]{:S(2)}) async-start(), calls=%async_computation.1 | async-start | bytes 4325376 | tf_op jit(solution)/shard_map/all_gather | solution.py:37
  9.7 310.8 %reduce-scatter.2.cloned.1.call-start = ((), (), s32[]{:S(2)}) async-start(), calls=%async_computation.2 | async-start | bytes 8650752 | tf_op jit(solution)/shard_map/reduce_scatter | solution.py:193
  125.2 17.5 %copy-start.2 = (bf16[512,512]{0,1:T(8,128)(2,1)S(1)}, bf16[512,512]{0,1:T(8,128)(2,1)}, u32[]{:S(2)}) copy-start(bf16[512,512]{0,1:T(8,128)(2,1)} %copy.48) | copy-start | bytes 1572868
  144.9 11.8 %copy-start.1 = (bf16[16,128,8,64]{1,3,2,0:T(8,128)(2,1)S(1)}, bf16[16,128,8,64]{1,3,2,0:T(8,128)(2,1)}, u32[]{:S(2)}) copy-start(bf16[16,128,8,64]{1,3,2,0:T(8,128)(2,1)} %gather_fusion.1) | copy-start | bytes 6291460
  144.9 11.8 %copy-start.4 = (f32[16,128,128]{2,1,0:T(8,128)S(1)}, f32[16,128,128]{2,1,0:T(8,128)}, u32[]{:S(2)}) copy-start(f32[16,128,128]{2,1,0:T(8,128)} %convert_multiply_fusion.2) | copy-start | bytes 3145732
  190.4 0.7 copy-start.8
  190.4 1.1 copy-start.3
  190.4 1.8 copy-start.5
  190.5 219.4 %all-reduce.4.cloned.1.call-start = ((), (), s32[]{:S(2)}) async-start(), calls=%async_computation.3 | async-start | bytes 524288 | tf_op jit(solution)/shard_map/psum | solution.py:194
  320.5 345.6 %all-reduce.6.cloned.1.call-start = ((), (), s32[]{:S(2)}) async-start(), calls=%async_computation.4 | async-start | bytes 524288 | tf_op jit(solution)/shard_map/psum | solution.py:199
Sparse Core Ops, SparseCore 0:
  10.5 69.7 all-gather.1
  190.6 129.8 reduce-scatter.1
  323.1 86.7 all-reduce.3
  416.6 249.4 all-reduce.5
where the time goes:
time: 682 us; the launch traced here: 675 us
  waiting for transfers between devices  443 us (65%)
  blocking collectives  75.9 us (11%)
  matrix products  70.5 us (10%)
  local copies, waits for them, and re-layouts  43.3 us (6%)
  other arithmetic  26.5 us (4%)
  between operations  15 us (2%)
    psum x1, waiting for transfers between devices, shards(): lax.psum((weight_part, att_src_part, att_dst_part), ('panel', 'rep'))  252 us
    reduce_scatter x1, waiting for transfers between devices, shards(): lax.psum_scatter(source_flat, 'panel', scatter_dimension=0, tiled=True)  122 us
    psum x1, blocking collectives, shards(): lax.psum((weight_part, att_src_part, att_dst_part), ('panel', 'rep'))  75.9 us
    all_gather x1, waiting for transfers between devices, shards(): proj_all = lax.all_gather(proj_own, 'panel', axis=0, tiled=True)  57.2 us
    another operation x2, local copies, waits for them, and re-layouts, shards(): source_feats.reshape(source_blocks, block_size, num_heads, head_dim)  20.2 us
    dot_general x1, matrix products, backward_group(): jnp.einsum('gihk,gjhk->ghij', cotan_rows, source_rows, preferred_element_...  15.4 us
  transfers between devices with their start and end apart: 4, of which 4 were waited for; matrix products, arithmetic and copies ran while one was open for 3% of the time, Pallas kernels for 0%

commit v1 on v0

--- a/solution.py
+++ b/solution.py
@@ -34,7 +34,8 @@
     source_local = x_src.shape[0]
     slot_count = block_rows.shape[0]
     proj_own = jnp.dot(x_src, weight, preferred_element_type=jnp.float32).astype(jnp.bfloat16)
-    proj_all = lax.all_gather(proj_own, "panel", axis=0, tiled=True)
+    sent = jnp.stack([proj_own] * lax.axis_size("panel"))
+    proj_all = jnp.concatenate(lax.all_to_all(sent, "panel", 0, 0), axis=0)
     source_total = proj_all.shape[0]
     dest_blocks = dest_count // block_size
     source_blocks = source_total // block_size

time: 682 us -> 705 us (1.034)
  waiting for transfers between devices: 443 us -> 472 us
  local copies, waits for them, and re-layouts: 43.3 us -> 31.6 us
  starting transfers between devices: 0.16 us -> 10.1 us
    all_to_all x0 -> x1, waiting for transfers between devices: none -> 89 us  [shards(): proj_all = jnp.concatenate(lax.all_to_all(sent, 'panel', 0, 0), axis=0)]
    all_gather x1 -> x0, waiting for transfers between devices: 57.2 us -> none  [shards(): proj_all = lax.all_gather(proj_own, 'panel', axis=0, tiled=True)]
    all_to_all x0 -> x1, starting transfers between devices: none -> 9.99 us  [shards(): proj_all = jnp.concatenate(lax.all_to_all(sent, 'panel', 0, 0), axis=0)]
    another operation x2, local copies, waits for them, and re-layouts: 20.2 us -> 10.7 us  [the longest x1 7.74 us: shards(): source_feats = proj_all.reshape(source_total, num_heads, head_dim)]
where the time goes in v1:
time: 705 us; the launch traced here: 698 us
  waiting for transfers between devices  472 us (67%)
  blocking collectives  75.2 us (11%)
  matrix products  68 us (10%)
  local copies, waits for them, and re-layouts  31.6 us (4%)
  other arithmetic  25.9 us (4%)
  between operations  15.1 us (2%)
  starting transfers between devices  10.1 us (1%)
    psum x1, waiting for transfers between devices, shards(): lax.psum((weight_part, att_src_part, att_dst_part), ('panel', 'rep'))  252 us
    reduce_scatter x1, waiting for transfers between devices, shards(): lax.psum_scatter(source_flat, 'panel', scatter_dimension=0, tiled=True)  119 us
    all_to_all x1, waiting for transfers between devices, shards(): proj_all = jnp.concatenate(lax.all_to_all(sent, 'panel', 0, 0), axis=0)  89 us
    psum x1, blocking collectives, shards(): lax.psum((weight_part, att_src_part, att_dst_part), ('panel', 'rep'))  75.2 us
    dot_general x1, matrix products, backward_group(): jnp.einsum('gihk,gjhk->ghij', cotan_rows, source_rows, preferred_element_...  16.1 us
  transfers between devices with their start and end apart: 4, of which 4 were waited for; matrix products, arithmetic and copies ran while one was open for 3% of the time, Pallas kernels for 0%

profile of v1, /device:TPU:2, one launch (start us, length us, event | category | flops | bytes accessed | tf_op | source)
XLA Modules:
  0.0 698.4 jit_solution(13731058129409394105)
XLA Ops:
  9.2 2.9 stack.2
  12.1 10.0 %all-to-all-start = ((bf16[32,128,512]{1,2,0:T(8,128)(2,1)}), bf16[32,128,512]{1,2,0:T(8,128)(2,1)}, u32[]{:S(2)}, u32[]{:S(2)}) async-start(bf16[32,128,512]{1,2,0:T(8,128)(2,1)} %stack.2), calls=%async_computation | async-start | bytes 8388608 | tf_op jit(solution)/shard_map/all_to_all | solution.py:38
  27.4 2.4 convert_multiply_fusion.2
  29.8 89.0 %all-to-all-done = bf16[32,128,512]{1,2,0:T(8,128)(2,1)} async-done(((bf16[32,128,512]{1,2,0:T(8,128)(2,1)}), bf16[32,128,512]{1,2,0:T(8,128)(2,1)}, u32[]{:S(2)}, u32[]{:S(2)}) %all-to-all-start) | async-done | bytes 4194336 | tf_op jit(solution)/shard_map/all_to_all | solution.py:38
  118.8 6.9 copy.41
  125.6 7.7 %reshape_reshape.7 = bf16[4096,8,64]{0,2,1:T(8,128)(2,1)} reshape(bf16[32,128,512]{1,0,2:T(8,128)(2,1)} %copy.41) | data formatting | bytes 8388608 | tf_op jit(solution)/shard_map/reshape;reshape | solution.py:42
  133.4 3.9 fusion.99
  137.7 9.5 %fusion.23 = f32[16,8,128]{2,1,0:T(8,128)S(1)} fusion(f32[16,128,128]{2,1,0:T(8,128)} %convert_multiply_fusion.2, f32[16,8,128]{2,1,0:T(8,128)S(1)} %copy.42, f32[16,8,128]{2,1,0:T(8,128)S(1)} %copy.39), kind=kLoop, calls=%fused_computation.33 | loop fusion | flops 25149440 | bytes 1245184 | tf_op jit(solution)/shard_map/while/body/eval_jaxpr/reduce_sum | solution.py:100
  147.4 4.3 gather_fusion.1
  151.7 9.5 %fusion.27 = f32[16,128,8,64]{1,3,2,0:T(8,128)S(1)} fusion(f32[16,128,128]{2,1,0:T(8,128)} %convert_multiply_fusion.2, f32[16,8,128]{2,1,0:T(8,128)} %copy-done.9, f32[16,8,128]{2,1,0:T(8,128)} %copy-done.7, bf16[16,128,8,64]{1,3,2,0:T(8,128)(2,1)} %gather_fusion.1, pred[16]{0:T(512)(128)(4,1)S(1)} %get-tuple-element.104), kind=kOutput, calls=%fused_computation.35 | convolution fusion | flops 294649856 | bytes 7471120 | tf_op jit(solution)/shard_map/while/body/eval_jaxpr/ghij,gjhk->gihk/dot_general | solution.py:93
  161.2 5.0 fusion.14
  166.2 2.6 reshape.106
  171.0 12.0 %fusion.24 = f32[16,128,8,64]{1,3,2,0:T(8,128)S(1)} fusion(f32[16,8,128]{2,1,0:T(8,128)S(1)} %copy.44, f32[16,128,128]{2,1,0:T(8,128)} %convert_multiply_fusion.2, f32[16,8,128]{2,1,0:T(8,128)} %copy-done.9, f32[16,8,128]{2,1,0:T(8,128)} %copy-done.7, bf16[16,128,8,64]{1,3,2,0:T(8,128)(2,1)S(1)} %gather_fusion, pred[16]{0:T(512)(128)(4,1)S(1)} %get-tuple-element.105), kind=kOutput, calls=%fused_computation.34 | convolution fusion | flops 296747008 | bytes 7536656 | tf_op jit(solution)/shard_map/while/body/eval_jaxpr/ghij,gihk->gjhk/dot_general | solution.py:144
  183.1 16.1 %fusion.96 = (f32[16,8,128]{2,1,0:T(8,128)}, f32[16,8,128]{2,1,0:T(8,128)S(1)}) fusion(f32[16,8,128]{2,1,0:T(8,128)S(1)} %copy.48, bf16[16,128,8,64]{1,3,2,0:T(8,128)(2,1)S(1)} %copy-done.1, pred[16]{0:T(512)(128)(4,1)S(1)} %get-tuple-element.104, bf16[16,128,8,64]{1,3,2,0:T(8,128)(2,1)S(1)} %gather_fusion, pred[16]{0:T(512)(128)(4,1)S(1)} %get-tuple-element.105, ...), kind=kOutput, calls=%fused_computation.128 | convolution fusion | flops 316637184 | bytes 5636128 | tf_op jit(solution)/shard_map/while/body/eval_jaxpr/gihk,gjhk->ghij/dot_general | solution.py:137
  199.6 5.8 fusion.16
  205.4 12.0 %bitcast_add_fusion = f32[4096,512]{0,1:T(8,128)} fusion(f32[64,8,32,128]{3,2,1,0:T(8,128)S(1)} %bitcast.178, f32[512]{0:T(512)S(1)} %mul.185, f32[4096,8]{0,1:T(8,128)S(1)} %bitcast.183), kind=kLoop, calls=%fused_computation.22 | loop fusion | flops 4194304 | bytes 16910336 | tf_op jit(solution)/shard_map/add | solution.py:182
  219.9 5.1 fusion.103
  225.0 119.2 %reduce-scatter.2.cloned.1.call-done = f32[128,512]{0,1:T(8,128)} async-done(((f32[4096,512]{0,1:T(8,128)}), f32[128,512]{0,1:T(8,128)}) %reduce-scatter.2.cloned.1.call-update) | async-done | bytes 262160 | tf_op jit(solution)/shard_map/reduce_scatter | solution.py:194
  344.7 75.2 %all-reduce = (f32[8,64]{1,0:T(8,128)}, f32[8,64]{1,0:T(8,128)}) all-reduce(f32[8,64]{1,0:T(8,128)S(1)} %add.168, f32[8,64]{1,0:T(8,128)S(1)} %bitcast.197), channel_id=1, replica_groups=mesh['panel'=32,'rep'=8] {'panel','rep'}, use_global_device_ids=true, to_apply=%region_8.10 | all-reduce | flops 1024 | bytes 8192 | tf_op jit(solution)/shard_map/psum | solution.py:200
  421.6 11.8 %all-reduce.4.cloned.1.call-done = f32[128,512]{0,1:T(8,128)} async-done(((f32[128,512]{0,1:T(8,128)}), f32[128,512]{0,1:T(8,128)}) %all-reduce.4.cloned.1.call-update) | async-done | bytes 262160 | tf_op jit(solution)/shard_map/psum | solution.py:195
  433.4 2.0 convolution_add_fusion
  435.5 2.0 fusion.101
  437.4 252.4 %all-reduce.6.cloned.1.call-done = f32[128,512]{0,1:T(8,128)} async-done(((f32[128,512]{0,1:T(8,128)}), f32[128,512]{0,1:T(8,128)}) %all-reduce.6.cloned.1.call-update) | async-done | bytes 262160 | tf_op jit(solution)/shard_map/psum | solution.py:200
  689.8 1.8 copy.52
  (81 shorter events, 14.2 us)
Async XLA Ops:
  7.2 0.9 copy-start
  7.2 15.0 %copy-start.3 = (bf16[512,512]{1,0:T(8,128)(2,1)S(1)}, bf16[512,512]{1,0:T(8,128)(2,1)}, u32[]{:S(2)}) copy-start(bf16[512,512]{1,0:T(8,128)(2,1)} %param.17) | copy-start | bytes 1572868
  7.2 16.5 %copy-start.5 = (bf16[512,128]{1,0:T(8,128)(2,1)S(1)}, bf16[512,128]{1,0:T(8,128)(2,1)}, u32[]{:S(2)}) copy-start(bf16[512,128]{1,0:T(8,128)(2,1)} %param.13) | copy-start | bytes 393220
  7.2 16.8 %copy-start.13 = (f32[8,64]{1,0:T(8,128)S(1)}, f32[8,64]{1,0:T(8,128)}, u32[]{:S(2)}) copy-start(f32[8,64]{1,0:T(8,128)} %param.16) | copy-start | bytes 6148
  9.1 15.3 %copy-start.12 = (s32[16]{0:T(128)S(1)}, s32[16]{0:T(128)}, u32[]{:S(2)}) copy-start(s32[16]{0:T(128)} %param.18) | copy-start | bytes 196
  9.1 16.8 %copy-start.11 = (f32[8,64]{1,0:T(8,128)S(1)}, f32[8,64]{1,0:T(8,128)}, u32[]{:S(2)}) copy-start(f32[8,64]{1,0:T(8,128)} %param.15) | copy-start | bytes 6148
  12.1 106.7 %all-to-all-start = ((bf16[32,128,512]{1,2,0:T(8,128)(2,1)}), bf16[32,128,512]{1,2,0:T(8,128)(2,1)}, u32[]{:S(2)}, u32[]{:S(2)}) async-start(bf16[32,128,512]{1,2,0:T(8,128)(2,1)} %stack.2), calls=%async_computation | async-start | bytes 8388608 | tf_op jit(solution)/shard_map/all_to_all | solution.py:38
  22.1 4.9 copy-start.14
  22.1 322.0 %reduce-scatter.2.cloned.1.call-start = ((), (), s32[]{:S(2)}) async-start(), calls=%async_computation.2 | async-start | bytes 8650752 | tf_op jit(solution)/shard_map/reduce_scatter | solution.py:194
  24.7 113.0 %copy-start.7 = (f32[16,8,128]{2,1,0:T(8,128)}, f32[16,8,128]{2,1,0:T(8,128)S(1)}, u32[]{:S(2)}) copy-start(f32[16,8,128]{2,1,0:T(8,128)S(1)} %copy.39) | copy-start | bytes 196612
  137.7 14.1 %copy-start.9 = (f32[16,8,128]{2,1,0:T(8,128)}, f32[16,8,128]{2,1,0:T(8,128)S(1)}, u32[]{:S(2)}) copy-start(f32[16,8,128]{2,1,0:T(8,128)S(1)} %copy.42) | copy-start | bytes 196612
  151.7 17.1 %copy-start.2 = (bf16[512,512]{0,1:T(8,128)(2,1)S(1)}, bf16[512,512]{0,1:T(8,128)(2,1)}, u32[]{:S(2)}) copy-start(bf16[512,512]{0,1:T(8,128)(2,1)} %copy.46) | copy-start | bytes 1572868
  171.0 12.1 %copy-start.1 = (bf16[16,128,8,64]{1,3,2,0:T(8,128)(2,1)S(1)}, bf16[16,128,8,64]{1,3,2,0:T(8,128)(2,1)}, u32[]{:S(2)}) copy-start(bf16[16,128,8,64]{1,3,2,0:T(8,128)(2,1)} %gather_fusion.1) | copy-start | bytes 6291460
  171.0 12.1 %copy-start.4 = (f32[16,128,128]{2,1,0:T(8,128)S(1)}, f32[16,128,128]{2,1,0:T(8,128)}, u32[]{:S(2)}) copy-start(f32[16,128,128]{2,1,0:T(8,128)} %convert_multiply_fusion.2) | copy-start | bytes 3145732
  171.0 12.1 %copy-start.8 = (f32[16,8,128]{2,1,0:T(8,128)S(1)}, f32[16,8,128]{2,1,0:T(8,128)}, u32[]{:S(2)}) copy-start(f32[16,8,128]{2,1,0:T(8,128)} %copy-done.7) | copy-start | bytes 196612
  171.0 12.1 %copy-start.10 = (f32[16,8,128]{2,1,0:T(8,128)S(1)}, f32[16,8,128]{2,1,0:T(8,128)}, u32[]{:S(2)}) copy-start(f32[16,8,128]{2,1,0:T(8,128)} %copy-done.9) | copy-start | bytes 196612
  217.4 0.8 copy-start.6
  217.5 216.0 %all-reduce.4.cloned.1.call-start = ((), (), s32[]{:S(2)}) async-start(), calls=%async_computation.3 | async-start | bytes 524288 | tf_op jit(solution)/shard_map/psum | solution.py:195
  344.2 345.7 %all-reduce.6.cloned.1.call-start = ((), (), s32[]{:S(2)}) async-start(), calls=%async_computation.4 | async-start | bytes 524288 | tf_op jit(solution)/shard_map/psum | solution.py:200
Sparse Core Ops, SparseCore 0:
  217.6 126.5 reduce-scatter.1
  346.7 86.6 all-reduce.3
  440.4 249.4 all-reduce.5
